TPU v7x, 32 devices: a whole 2x2x4 slice. The times are simulated.
32 devices in a mesh: seq: 4 (over y, core), head: 8 (over z, x).
Axes of the slice: x: 2, y: 2, z: 4, core: 2. Of those that a mesh axis runs over, the one named last changes fastest.
Arguments:
- tokens: bfloat16 [4096, 6144], P('seq', 'head'), may hold values from -6 to 6
- proj_weight: bfloat16 [4, 6144, 1024], P(None, None, 'head'), may hold values from -0.078125 to 0.078125
- decay_rate: float32 [1024], P('head'), may hold values from 5e-05 to 0.04
- norm_gain: float32 [1024], P('head'), may hold values from 0.5 to 1.5
- pool_down: bfloat16 [16, 6144, 64], P('head'), may hold values from -0.078125 to 0.078125
- pool_up: bfloat16 [16, 64, 1024], P('head'), may hold values from -0.75 to 0.75
- span_id: int32 [4, 2], replicated, may hold values from 0 to 7, as said below
- prompt_adapter: int32 [8], replicated, may hold values from 0 to 15
- owner_pos: int32 [16], replicated, may hold values from 0 to 15, each once
- slice_len: int32 [4, 2], replicated, may hold values from 1 to 512, as said below
Outputs:
- mixed_out: bfloat16 [4096, 1024], P('seq', 'head')
- end_states: float32 [4, 2, 1024, 128], P('seq', None, 'head')
Inputs may be any that keep to these rules, and one draw needn't show every extreme that they name: `span_id`: along each lane, the slices of one prompt stand on consecutive seq indices and share an id; a prompt holds 1 to 4 slices; ids of different lanes differ. `slice_len`: A slice followed in its lane by a slice of the same prompt holds 512 tokens. `owner_pos`: each pool position holds exactly one adapter.
All inputs are finite; a program needn't handle non-finite values.
Results may differ from a plain program's by a relative error of at most 0.002.
The roundings to bfloat16 on the way count: a program that leaves them out, or rounds other values in their place, can miss the bound.
Values may be sent and summed in bfloat16 or wider, within the bound.
A program may use at most 128 MiB of HBM per device.

v0:
```python
import jax
import jax.numpy as jnp
from jax import lax
from jax.sharding import PartitionSpec as P

P_SIZE = 128


NORM_FLOOR = 1.0


def broadcast(block, axis, source):
    block = jnp.where(lax.axis_index(axis) == source, block, jnp.zeros_like(block))
    return lax.psum(block, axis)


def entering(array, axis, combine, identity):
    length, here = (lax.axis_size(axis), lax.axis_index(axis))
    everything = jax.tree.map(lambda part: lax.all_gather(part, axis), array)
    start = jax.tree.map(
        lambda part, zero: jnp.broadcast_to(jnp.asarray(zero, part.dtype), part.shape),
        array,
        identity,
    )

    def turn(k, before):
        reached = k < here
        new = combine(before, jax.tree.map(lambda part: part[k], everything))
        return jax.tree.map(lambda a, b: jnp.where(reached, a, b), new, before)

    return lax.fori_loop(0, length, turn, start)


def lookup(values, table):
    positions = jnp.arange(table.shape[0], dtype=jnp.int32)
    return jnp.sum(jnp.where(values[:, None] == positions[None, :], table[None, :], 0), axis=1)


def compose(earlier, later):
    early_keep, early_decay, early_state = earlier
    late_keep, late_decay, late_state = later
    factor = late_keep[:, None, None, None] * late_decay[..., None]
    return (early_keep * late_keep, early_decay * late_decay, factor * early_state + late_state)


def body(
    tokens,
    proj_weight,
    decay_rate,
    norm_gain,
    pool_down,
    pool_up,
    span_id,
    prompt_adapter,
    owner_pos,
    slice_len,
):
    lanes = span_id.shape[1]
    slice_rows = tokens.shape[0] // lanes
    head_width = proj_weight.shape[2]
    heads_here = head_width // P_SIZE
    seq_index = lax.axis_index("seq")
    head_index = lax.axis_index("head")
    own_span = lax.dynamic_index_in_dim(span_id, seq_index, 0, keepdims=False)
    prior_span = lax.dynamic_index_in_dim(span_id, jnp.maximum(seq_index - 1, 0), 0, keepdims=False)
    keep_flag = jnp.where((seq_index > 0) & (own_span == prior_span), 1.0, 0.0).astype(jnp.float32)
    self_span_length = lax.dynamic_index_in_dim(slice_len, seq_index, 0, keepdims=False)
    places = lookup(lookup(own_span, prompt_adapter), owner_pos)
    per_owner = pool_down.shape[0]
    owners = places // per_owner
    local_slot = places % per_owner
    down_local = jnp.take(pool_down, local_slot, axis=0)
    up_local = jnp.take(pool_up, local_slot, axis=0)
    down_list = []
    up_list = []
    for lane_pos in range(lanes):
        fetched = (
            broadcast(down_local[lane_pos], "head", owners[lane_pos]),
            broadcast(up_local[lane_pos], "head", owners[lane_pos]),
        )
        down_list.append(fetched[0])
        up_list.append(fetched[1])
    down_stack = jnp.stack(down_list)
    up_stack = jnp.stack(up_list)
    up_projection_columns = lax.dynamic_slice_in_dim(
        up_stack, head_index * head_width, head_width, 2
    )
    shard_piece = lax.all_gather(tokens, "head", axis=1, tiled=True)
    count = shard_piece.shape[1]
    proj_sum = jnp.einsum(
        "td,kdc->tkc", shard_piece, proj_weight, preferred_element_type=jnp.float32
    )
    low_sum = jnp.einsum(
        "gmn,gna->gma",
        shard_piece.reshape(lanes, slice_rows, count),
        down_stack,
        preferred_element_type=jnp.float32,
    )
    proj_sum, low_sum = (proj_sum, low_sum)
    shape_four = (lanes, slice_rows, heads_here, P_SIZE)
    query = proj_sum[:, 0].astype(jnp.bfloat16)
    key_unprocessed = proj_sum[:, 1].astype(jnp.bfloat16)
    value = proj_sum[:, 2].astype(jnp.bfloat16)
    lower_rank_part = low_sum.astype(jnp.bfloat16)
    gate = proj_sum[:, 3].reshape(lanes, slice_rows, head_width) + jnp.einsum(
        "evp,epq->evq", lower_rank_part, up_projection_columns, preferred_element_type=jnp.float32
    )
    slot_ids = jnp.arange(slice_rows, dtype=jnp.int32)
    live = (slot_ids[None, :] < self_span_length[:, None]).astype(jnp.float32)
    step_log = -(live[..., None] * decay_rate[None, None, :] * (2.0 * jax.nn.sigmoid(gate)))
    cumul = jnp.cumsum(step_log, axis=1).reshape(shape_four)
    query_f = query.astype(jnp.float32).reshape(shape_four)
    key_f = (
        key_unprocessed.astype(jnp.float32).reshape(shape_four)
        * (live * P_SIZE ** (-0.5))[:, :, None, None]
    )
    value_f = value.astype(jnp.float32).reshape(shape_four)
    query_decay = query_f * jnp.exp(cumul)
    key_decay = key_f * jnp.exp(-cumul)
    causal = slot_ids[:, None] >= slot_ids[None, :]
    attention_scores = jnp.einsum(
        "lthc,ljhc->lhtj", query_decay, key_decay, precision=lax.Precision.HIGHEST
    )
    attention_scores = jnp.where(causal[None, None], attention_scores, 0.0)
    inner = jnp.einsum(
        "lhtj,ljhd->lthd", attention_scores, value_f, precision=lax.Precision.HIGHEST
    )
    last_cumul = cumul[:, -1]
    decay_end = jnp.exp(last_cumul)
    carried = jnp.einsum(
        "ljhc,ljhd->lhcd",
        key_f * jnp.exp(last_cumul[:, None] - cumul),
        value_f,
        precision=lax.Precision.HIGHEST,
    )
    identity = (jnp.ones_like(keep_flag), jnp.ones_like(decay_end), jnp.zeros_like(carried))
    prefix = entering((keep_flag, decay_end, carried), "seq", compose, identity)
    incoming = prefix[2]
    start_state = keep_flag[:, None, None, None] * incoming
    inner = inner + jnp.einsum(
        "lthc,lhcd->lthd", query_decay, start_state, precision=lax.Precision.HIGHEST
    )
    normed = (
        inner
        * lax.rsqrt(jnp.maximum(jnp.mean(inner * inner, axis=-1, keepdims=True), NORM_FLOOR))
        * norm_gain.reshape(heads_here, P_SIZE)
    )
    mixed_out = (
        (normed * live[:, :, None, None])
        .reshape(lanes * slice_rows, head_width)
        .astype(jnp.bfloat16)
    )
    end_states = decay_end[..., None] * start_state + carried
    return (mixed_out, end_states.reshape(1, lanes, head_width, P_SIZE))


def solution(mesh):
    in_specs = (
        P("seq", "head"),
        P(None, None, "head"),
        P("head"),
        P("head"),
        P("head", None, None),
        P("head", None, None),
        P(),
        P(),
        P(),
        P(),
    )
    out_specs = (P("seq", "head"), P("seq", None, "head", None))
    return jax.shard_map(body, mesh=mesh, in_specs=in_specs, out_specs=out_specs, check_vma=False)
```

profile of v0, /device:TPU:1, one launch (start us, length us, event | category | flops | bytes accessed | tf_op | source)
XLA Modules:
  0.0 332.6 jit_solution(6812111788907914241)
XLA Ops:
  7.2 0.7 all-gather.5.cloned.1.call-update
  8.0 1.0 fusion.58
  8.9 0.8 fusion.54
  9.8 0.8 fusion.55
  10.6 0.6 fusion.66
  12.6 0.6 gather_fusion
  13.2 1.5 gather_fusion.1
  14.8 0.1 broadcast_select_fusion.1
  14.9 0.7 slice_select_fusion.2
  15.6 0.2 broadcast_select_fusion
  15.8 1.3 slice_select_fusion.1
  17.1 0.7 fusion.45
  17.9 0.8 iota_compare_fusion
  18.7 0.1 copy.73
  18.8 0.2 fusion.56
  19.0 6.3 %all-gather.2 = f32[4,1,2]{2,1,0:T(1,128)} all-gather(f32[1,1,2]{2,1,0:T(1,128)S(1)} %bitcast.109), channel_id=1, replica_groups=mesh['seq'=4,'head'=8] {'seq'}, dimensions={0}, use_global_device_ids=true | all-gather | bytes 40 | tf_op jit(solution)/shard_map/all_gather | solution.py:19
  25.3 162.9 %all-gather.5.cloned.1.call-done = bf16[1024,6144]{1,0:T(8,128)(2,1)} async-done(((bf16[1024,768]{1,0:T(8,128)(2,1)}), bf16[1024,6144]{1,0:T(8,128)(2,1)}) %all-gather.5.cloned.1.call-update) | async-done | bytes 12582928 | tf_op jit(solution)/shard_map/all_gather | solution.py:88
  188.1 12.3 %fusion.67 = (bf16[1024,4,128]{2,0,1:T(8,128)(2,1)}, f32[1024,4,128]{2,0,1:T(8,128)S(1)}) fusion(bf16[4,6144,128]{2,1,0:T(8,128)(2,1)} %param.13, bf16[1024,6144]{1,0:T(8,128)(2,1)} %all-gather.5.cloned.1.call-done), kind=kOutput, calls=%fused_computation.106 | convolution fusion | flops 6442975232 | bytes 22020096 | tf_op jit(solution)/shard_map/td,kdc->tkc/dot_general | solution.py:90
  200.5 87.9 %all-reduce.3.cloned.1.call-done = (bf16[1,6144,64]{1,2,0:T(8,128)(2,1)}, bf16[1,6144,64]{1,2,0:T(8,128)(2,1)}, bf16[1,64,1024]{2,1,0:T(8,128)(2,1)}, bf16[1,64,1024]{2,1,0:T(8,128)(2,1)}) async-done(((bf16[1,6144,64]{1,2,0:T(8,128)(2,1)}, bf16[1,6144,64]{1,2,0:T(8,128)(2,1)}, bf16[1,64,1024]{2,1,0:T(8,128)(2,1)}, bf16[1,64,1024]{2,1,0:T(8,128)(2,1)}), (bf16[1,6144,64]{1,2,0:T(8,128)(2,1)}, ...) | async-done | bytes 1835024 | tf_op jit(solution)/shard_map/psum | solution.py:14
  288.4 9.3 %fusion.22 = f32[2,512,128]{2,1,0:T(8,128)S(1)} fusion(f32[2,512,128]{2,1,0:T(8,128)S(1)} %bitcast.100, bf16[2,512,6144]{2,1,0:T(8,128)(2,1)} %bitcast.94, bf16[1,6144,64]{1,2,0:T(8,128)(2,1)} %get-tuple-element.183, bf16[1,6144,64]{1,2,0:T(8,128)(2,1)} %get-tuple-element.184, f32[128]{0:T(128)S(1)} %copy-done.8, f32[2,512]{1,0:T(2,128)S(1)} %copy.73, ...), kind=kOutput, calls=%fused_computation.25 | convolution fusion | flops 824049664 | bytes 15471108 | tf_op jit(solution)/shard_map/evp,epq->evq/dot_general | solution.py:105
  297.6 0.3 fusion.39
  298.0 0.1 broadcast_add_fusion
  298.2 0.4 copy.116
  298.6 0.6 fusion.64
  299.4 5.3 %all-gather = f32[8,1,1,128]{3,2,1,0:T(1,128)S(1)} all-gather(f32[2,1,1,128]{3,2,1,0:T(1,128)S(1)} %bitcast.108), channel_id=2, replica_groups=mesh['seq'=4,'head'=8] {'seq'}, dimensions={0}, use_global_device_ids=true | all-gather | bytes 5120 | tf_op jit(solution)/shard_map/all_gather | solution.py:19
  304.7 2.5 fusion.32
  307.2 0.6 fusion.35
  307.8 0.6 copy-done.1
  308.5 7.8 %all-gather.1 = f32[8,128,128]{2,1,0:T(8,128)S(1)} all-gather(f32[2,128,128]{2,1,0:T(8,128)S(1)} %fusion.35), channel_id=3, replica_groups=mesh['seq'=4,'head'=8] {'seq'}, dimensions={0}, use_global_device_ids=true | all-gather | bytes 655360 | tf_op jit(solution)/shard_map/all_gather | solution.py:19
  316.3 3.6 %while.14 = (s32[]{:T(128)}, f32[2,1,128,128]{3,2,1,0:T(8,128)S(1)}, s32[]{:T(128)}, f32[4,2]{1,0:T(4,128)}, f32[4,2,1,128]{3,1,2,0:T(2,128)S(1)}, /*index=5*/f32[4,2,1,128,128]{4,3,1,2,0:T(8,128)S(1)}, s32[]{:T(128)}, s32[]{:T(128)}) while((s32[]{:T(128)}, f32[2,1,128,128]{3,2,1,0:T(8,128)S(1)}, s32[]{:T(128)}, ...), condition=%wide.region_9.10_spmd.clone, body=%wide.region_8.9_spmd.clone.sunk | while | flops 131332 | bytes 396437 | solution.py:31
  316.3 0.7 fusion.74
  317.0 0.1 bitcast_multiply_fusion.4
  317.0 0.1 fusion.75
  317.2 0.7 fusion.74
  317.9 0.1 bitcast_multiply_fusion.4
  317.9 0.1 fusion.75
  318.1 0.7 fusion.74
  318.8 0.1 bitcast_multiply_fusion.4
  318.8 0.1 fusion.75
  319.0 0.7 fusion.74
  319.7 0.1 bitcast_multiply_fusion.4
  319.8 0.1 fusion.75
  319.9 1.8 fusion.37
  321.7 0.7 fusion.41
  322.5 1.5 multiply_reduce_fusion
  324.0 0.1 fusion.44
  324.1 0.8 copy.92
  325.0 0.8 fusion.47
  (39 shorter events, 0.5 us)
Async XLA Ops:
  7.2 5.4 %copy-start = (bf16[2,6144,64]{1,2,0:T(8,128)(2,1)S(1)}, bf16[2,6144,64]{1,2,0:T(8,128)(2,1)}, u32[]{:S(2)}) copy-start(bf16[2,6144,64]{1,2,0:T(8,128)(2,1)} %param.16) | copy-start | bytes 4718596
  7.2 181.0 %all-gather.5.cloned.1.call-start = ((), (), s32[]{:S(2)}) async-start(), calls=%async_computation | async-start | bytes 14155776 | tf_op jit(solution)/shard_map/all_gather | solution.py:88
  7.9 280.4 %all-reduce.3.cloned.1.call-start = ((), (), s32[]{:S(2)}) async-start(), calls=%async_computation.1 | async-start | bytes 3670016 | tf_op jit(solution)/shard_map/psum | solution.py:14
  17.1 1.7 copy-start.6
  25.3 263.1 %copy-start.8 = (f32[128]{0:T(128)S(1)}, f32[128]{0:T(128)}, u32[]{:S(2)}) copy-start(f32[128]{0:T(128)} %param.14) | copy-start | bytes 1540
  298.0 1.2 copy-start.5
  298.2 6.5 %copy-start.4 = (f32[2,512]{0,1:T(8,128)S(1)}, f32[2,512]{0,1:T(8,128)}, u32[]{:S(2)}) copy-start(f32[2,512]{0,1:T(8,128)} %fusion.45) | copy-start | bytes 12292
  307.8 0.7 copy-start.1
  319.9 2.5 copy-start.3
  322.4 1.6 copy-start.9
  322.4 2.5 copy-start.2
  322.5 2.5 copy-start.7
Sparse Core Ops, SparseCore 0:
  10.2 177.8 all-gather.4
  192.6 95.6 all-reduce.2
where the time goes:
time: 333 us
  waiting for transfers between devices  251 us (75%)
  matrix products  26.2 us (8%)
  blocking collectives  19.4 us (6%)
  between operations  15.6 us (5%)
  other arithmetic  10.5 us (3%)
  local copies, waits for them, and re-layouts  9.22 us (3%)
    all_gather x1, waiting for transfers between devices, body(): shard_piece = lax.all_gather(tokens, 'head', axis=1, tiled=True)  163 us
    psum x1, waiting for transfers between devices, broadcast(): return lax.psum(block, axis)  87.9 us
    all_gather x3, blocking collectives, entering(): everything = jax.tree.map(lambda part: lax.all_gather(part, axis), array)  19.4 us
    dot_general x1, matrix products, body(): jnp.einsum('td,kdc->tkc', shard_piece, proj_weight, preferred_element_typ...  12.3 us
    dot_general x1, matrix products, body(): jnp.einsum('evp,epq->evq', lower_rank_part, up_projection_columns, prefer...  9.27 us
  transfers between devices with their start and end apart: 2, of which 2 were waited for; matrix products, arithmetic and copies ran while one was open for 7% of the time, Pallas kernels for 0%

commit v1 on v0

v1 whole, which is shorter than its diff:
```python
import functools
import math

import jax
import jax.numpy as jnp
from jax import lax
from jax.experimental import pallas as pl
from jax.experimental.pallas import tpu as pltpu
from jax.sharding import PartitionSpec as P

P_SIZE = 128
NORM_FLOOR = 1.0
PIECES = 4
MESH = pl.DeviceIdType.MESH
HIGHEST = lax.Precision.HIGHEST


def grid_of(n):
    across = math.isqrt(n // 2)
    if across >= 2 and 2 * across * across == n:
        return across, n // across
    return 1, n


def head_at(position, n):
    across, depth = grid_of(n)
    if across == 1:
        return position
    width = across - 1
    back = lax.div(lax.div(position, depth) + (across - 1), across)
    rest = (position - depth) * back
    row, step = lax.div(rest, width), lax.rem(rest, width)
    x = 1 + step + lax.rem(row, 2) * (width - 1 - 2 * step)
    return (1 - back) * position * across + back * ((depth - 1 - row) * across + x)


def position_of(head, n):
    across, depth = grid_of(n)
    if across == 1:
        return head
    width = across - 1
    z, x = lax.div(head, across), lax.rem(head, across)
    back = lax.div(x + across - 1, across)
    row, step = depth - 1 - z, (x - 1) * back
    moved = step + lax.rem(row, 2) * (width - 1 - 2 * step)
    return (1 - back) * z + back * (depth + row * width + moved)


def dot(a, b, precision=None):
    return jnp.dot(a, b, preferred_element_type=jnp.float32, precision=precision)


def kernel(
    n,
    n_seq,
    span_ref,
    prompt_ref,
    owner_ref,
    len_ref,
    tok_ref,
    w_hbm,
    down_hbm,
    up_ref,
    rate_ref,
    gain_ref,
    out_ref,
    state_ref,
    slots,
    wbuf,
    dbuf,
    acc,
    lacc,
    up_send,
    up_recv,
    low_send,
    low_recv,
    low_full,
    st_send,
    st_recv,
    w_sem,
    ring_send,
    ring_recv,
    up_ssem,
    up_rsem,
    rs_ssem,
    rs_rsem,
    ag_ssem,
    ag_rsem,
    st_ssem,
    st_rsem,
):
    me = lax.axis_index("head")
    seq = lax.axis_index("seq")
    rows, shard = tok_ref.shape
    lanes = span_ref.shape[1]
    per_owner = down_hbm.shape[0]
    rank = down_hbm.shape[2]
    slice_rows = rows // lanes
    piece = rows // PIECES
    half = n // 2
    here = position_of(me, n)
    right = head_at(lax.rem(here + 1, n), n)
    left = head_at(lax.rem(here + n - 1, n), n)
    toward = (right, left)

    loads = [
        pltpu.make_async_copy(w_hbm.at[c], wbuf.at[:, pl.ds(c * P_SIZE, P_SIZE)], w_sem.at[c])
        for c in range(4)
    ]
    loads.append(pltpu.make_async_copy(down_hbm, dbuf, w_sem.at[4]))

    barrier = pltpu.get_barrier_semaphore()

    def greet_head(d, carry):
        pl.semaphore_signal(
            barrier, inc=1, device_id={"head": lax.rem(me + d, n)}, device_id_type=MESH
        )
        return carry

    def greet_seq(d, carry):
        pl.semaphore_signal(
            barrier, inc=1, device_id={"seq": lax.rem(seq + d, n_seq)}, device_id_type=MESH
        )
        return carry

    lax.fori_loop(1, n, greet_head, 0)
    lax.fori_loop(1, n_seq, greet_seq, 0)
    for load in loads:
        load.start()
    pl.semaphore_wait(barrier, n - 1 + n_seq - 1)

    def hop(direction, step, p, own=False):
        span = pl.ds(p * piece, piece)
        source = tok_ref.at[span] if own else slots.at[direction, step - 2, span]
        return pltpu.make_async_remote_copy(
            src_ref=source,
            dst_ref=slots.at[direction, step - 1, span],
            send_sem=ring_send.at[direction, step - 1, p],
            recv_sem=ring_recv.at[direction, step - 1, p],
            device_id={"head": toward[direction]},
            device_id_type=MESH,
        )

    def long_way(direction, p):
        return p % 2 == direction

    for k in range(PIECES):
        for direction in range(2):
            hop(direction, 1, (k + direction) % PIECES, own=True).start()

    places = [owner_ref[prompt_ref[span_ref[seq, j]]] for j in range(lanes)]
    owned = [
        [jnp.where(places[j] == me * per_owner + s, 1.0, 0.0).astype(jnp.float32) for s in range(per_owner)]
        for j in range(lanes)
    ]

    for j in range(lanes):
        mine = sum(owned[j][s] * up_ref[s].astype(jnp.float32) for s in range(per_owner)).astype(jnp.bfloat16)
        for i in range(n):
            up_send[i, pl.ds(j * rank, rank), :] = mine[:, i * P_SIZE : (i + 1) * P_SIZE]

    def up_copy(d):
        peer = lax.rem(me + d, n)
        return pltpu.make_async_remote_copy(
            src_ref=up_send.at[peer],
            dst_ref=up_recv.at[d],
            send_sem=up_ssem.at[d],
            recv_sem=up_rsem.at[d],
            device_id={"head": peer},
            device_id_type=MESH,
        )

    def up_start(d, carry):
        up_copy(d).start()
        return carry

    lax.fori_loop(1, n, up_start, 0)
    up_recv[0] = up_send[me]

    for load in loads:
        load.wait()

    def multiply(x, span, origin, first=False):
        deep = pl.ds(pl.multiple_of(origin * shard, 64), shard)
        gained = dot(x, wbuf[deep, :])
        lows = [dot(x, dbuf[s, deep, :]) for s in range(per_owner)]
        if first:
            acc[span, :] = gained
            for s in range(per_owner):
                lacc[s, span, :] = lows[s]
        else:
            acc[span, :] += gained
            for s in range(per_owner):
                lacc[s, span, :] += lows[s]

    def own_piece(p, carry):
        span = pl.ds(pl.multiple_of(p * piece, piece), piece)
        multiply(tok_ref[span, :], span, me, first=True)
        return carry

    lax.fori_loop(0, PIECES, own_piece, 0)

    def arrive(step, forward, present):
        order = [((k + d) % PIECES, d) for k in range(PIECES) for d in range(2)]
        order = [(p, d) for p, d in order if present(d, p)]
        for p, d in order:
            hop(d, step, p).wait_recv() if not isinstance(step, int) or step > 1 else hop(d, 1, p, own=True).wait_recv()
            if forward(d, p):
                hop(d, step + 1, p).start()
            sign = n - step if d == 0 else step
            origin = head_at(lax.rem(here + sign, n), n)
            span = pl.ds(p * piece, piece)
            multiply(slots[d, step - 1, span, :], span, origin)

    everything = lambda d, p: True
    nothing = lambda d, p: False
    if half >= 2:
        arrive(1, everything if half > 2 else long_way, everything)
    if half > 3:

        def middle(step, carry):
            arrive(step, everything, everything)
            return carry

        lax.fori_loop(2, half - 1, middle, 0)
    if half > 2:
        arrive(half - 1, long_way, everything)
    arrive(half, nothing, long_way)

    width = lanes * rank
    for j in range(lanes):
        span = pl.ds(j * slice_rows, slice_rows)
        mine = sum(owned[j][s] * lacc[s, span, :] for s in range(per_owner)).astype(jnp.bfloat16)
        low_send[:, pl.ds(j * rank, rank)] = mine
    block = slice_rows // n

    def rs_copy(d):
        peer = lax.rem(me + d, n)
        return pltpu.make_async_remote_copy(
            src_ref=low_send.at[pl.ds(pl.multiple_of(peer * block, block), block)],
            dst_ref=low_recv.at[d],
            send_sem=rs_ssem.at[d],
            recv_sem=rs_rsem.at[d],
            device_id={"head": peer},
            device_id_type=MESH,
        )

    def ag_copy(d):
        peer = lax.rem(me + d, n)
        return pltpu.make_async_remote_copy(
            src_ref=low_recv.at[0],
            dst_ref=low_full.at[me],
            send_sem=ag_ssem.at[d],
            recv_sem=ag_rsem.at[d],
            device_id={"head": peer},
            device_id_type=MESH,
        )

    def ag_arrival(d):
        peer = lax.rem(me + n - d, n)
        return pltpu.make_async_remote_copy(
            src_ref=low_recv.at[0],
            dst_ref=low_full.at[peer],
            send_sem=ag_ssem.at[d],
            recv_sem=ag_rsem.at[d],
            device_id={"head": peer},
            device_id_type=MESH,
        )

    def each(count, act):
        def turn(d, carry):
            act(d)
            return carry

        lax.fori_loop(1, count, turn, 0)

    each(n, lambda d: rs_copy(d).start())
    each(n, lambda d: up_copy(d).wait_recv())
    up = jnp.sum(up_recv[...].astype(jnp.float32), axis=0).astype(jnp.bfloat16)
    total = low_send[pl.ds(pl.multiple_of(me * block, block), block), :].astype(jnp.float32)
    each(n, lambda d: rs_copy(d).wait_recv())
    for d in range(1, n):
        total = total + low_recv[d].astype(jnp.float32)
    low_recv[0] = total.astype(jnp.bfloat16)
    each(n, lambda d: ag_copy(d).start())
    low_full[me] = total.astype(jnp.bfloat16)

    slot_ids = lax.broadcasted_iota(jnp.int32, (slice_rows, 1), 0)
    causal = lax.broadcasted_iota(jnp.int32, (slice_rows, slice_rows), 0) >= lax.broadcasted_iota(
        jnp.int32, (slice_rows, slice_rows), 1
    )
    triangle = jnp.where(causal, 1.0, 0.0).astype(jnp.float32)
    columns = lax.broadcasted_iota(jnp.int32, (1, width), 1)
    each(n, lambda d: ag_arrival(d).wait_recv())
    low = low_full[...].reshape(slice_rows, width).astype(jnp.float32)

    kept = []
    for j in range(lanes):
        span = pl.ds(j * slice_rows, slice_rows)
        own = (columns >= j * rank) & (columns < (j + 1) * rank)
        gate = acc[span, pl.ds(3 * P_SIZE, P_SIZE)] + dot(jnp.where(own, low, 0.0).astype(jnp.bfloat16), up)
        live = jnp.where(slot_ids < len_ref[seq, j], 1.0, 0.0).astype(jnp.float32)
        step_log = -(live * rate_ref[...] * (2.0 * jax.nn.sigmoid(gate)))
        cumul = dot(triangle, step_log, HIGHEST)
        query = acc[span, pl.ds(0, P_SIZE)].astype(jnp.bfloat16).astype(jnp.float32)
        key = acc[span, pl.ds(P_SIZE, P_SIZE)].astype(jnp.bfloat16).astype(jnp.float32) * (
            live * P_SIZE ** (-0.5)
        )
        value = acc[span, pl.ds(2 * P_SIZE, P_SIZE)].astype(jnp.bfloat16).astype(jnp.float32)
        last = cumul[slice_rows - 1 :, :]
        carried = lax.dot_general(
            key * jnp.exp(last - cumul),
            value,
            (((0,), (0,)), ((), ())),
            precision=HIGHEST,
            preferred_element_type=jnp.float32,
        )
        st_send[j, pl.ds(0, P_SIZE), :] = carried
        st_send[j, pl.ds(P_SIZE, 8), :] = jnp.broadcast_to(jnp.exp(last), (8, P_SIZE))
        kept.append((live, query * jnp.exp(cumul), key * jnp.exp(-cumul), value))

    def st_copy(d):
        return pltpu.make_async_remote_copy(
            src_ref=st_send,
            dst_ref=st_recv.at[seq],
            send_sem=st_ssem.at[d],
            recv_sem=st_rsem.at[d],
            device_id={"seq": lax.rem(seq + d, n_seq)},
            device_id_type=MESH,
        )

    def st_arrival(d):
        peer = lax.rem(seq + n_seq - d, n_seq)
        return pltpu.make_async_remote_copy(
            src_ref=st_send,
            dst_ref=st_recv.at[peer],
            send_sem=st_ssem.at[d],
            recv_sem=st_rsem.at[d],
            device_id={"seq": peer},
            device_id_type=MESH,
        )

    each(n_seq, lambda d: st_copy(d).start())
    st_recv[seq] = st_send[...]

    inners = []
    for j in range(lanes):
        live, query_decay, key_decay, value = kept[j]
        scores = lax.dot_general(
            query_decay,
            key_decay,
            (((1,), (1,)), ((), ())),
            precision=HIGHEST,
            preferred_element_type=jnp.float32,
        )
        inners.append(dot(jnp.where(causal, scores, 0.0), value, HIGHEST))

    each(n_seq, lambda d: st_arrival(d).wait_recv())
    for j in range(lanes):
        live, query_decay, _, _ = kept[j]
        span = pl.ds(j * slice_rows, slice_rows)
        ended = jnp.zeros((P_SIZE, P_SIZE), jnp.float32)
        start = ended
        final = ended
        for k in range(n_seq):
            if k:
                same = jnp.where(span_ref[k, j] == span_ref[k - 1, j], 1.0, 0.0).astype(jnp.float32)
                begun = same * ended
            else:
                begun = ended
            decay = jnp.broadcast_to(st_recv[k, j, pl.ds(P_SIZE, 1), :], (P_SIZE, P_SIZE)).T
            ended = decay * begun + st_recv[k, j, pl.ds(0, P_SIZE), :]
            at = jnp.where(seq == k, 1.0, 0.0).astype(jnp.float32)
            start = start + at * begun
            final = final + at * ended
        inner = inners[j] + dot(query_decay, start, HIGHEST)
        scale = lax.rsqrt(jnp.maximum(jnp.mean(inner * inner, axis=-1, keepdims=True), NORM_FLOOR))
        out_ref[span, :] = (inner * scale * gain_ref[...] * live).astype(jnp.bfloat16)
        state_ref[0, j] = final

    each(n, lambda d: up_copy(d).wait_send())
    each(n, lambda d: rs_copy(d).wait_send())
    each(n, lambda d: ag_copy(d).wait_send())
    each(n_seq, lambda d: st_copy(d).wait_send())
    for p in range(PIECES):
        for direction in range(2):
            hop(direction, 1, p, own=True).wait_send()
    for direction in range(2):
        for p in range(PIECES):
            reach = half if long_way(direction, p) else half - 1

            def drained(step, carry):
                hop(direction, step, p).wait_send()
                return carry

            lax.fori_loop(2, reach + 1, drained, 0)


def solution(mesh):
    n, n_seq = mesh.shape["head"], mesh.shape["seq"]

    def body(
        tokens,
        proj_weight,
        decay_rate,
        norm_gain,
        pool_down,
        pool_up,
        span_id,
        prompt_adapter,
        owner_pos,
        slice_len,
    ):
        rows, shard = tokens.shape
        model = proj_weight.shape[1]
        lanes = span_id.shape[1]
        per_owner, _, rank = pool_down.shape
        slice_rows = rows // lanes
        width = lanes * rank
        smem = pl.BlockSpec(memory_space=pltpu.SMEM)
        vmem = pl.BlockSpec(memory_space=pltpu.VMEM)
        hbm = pl.BlockSpec(memory_space=pl.ANY)
        dma = pltpu.SemaphoreType.DMA
        return pl.pallas_call(
            functools.partial(kernel, n, n_seq),
            out_shape=(
                jax.ShapeDtypeStruct((rows, P_SIZE), jnp.bfloat16),
                jax.ShapeDtypeStruct((1, lanes, P_SIZE, P_SIZE), jnp.float32),
            ),
            in_specs=[smem, smem, smem, smem, vmem, hbm, hbm, vmem, vmem, vmem],
            out_specs=(vmem, vmem),
            scratch_shapes=[
                pltpu.VMEM((2, n // 2, rows, shard), jnp.bfloat16),
                pltpu.VMEM((model, 4 * P_SIZE), jnp.bfloat16),
                pltpu.VMEM((per_owner, model, rank), jnp.bfloat16),
                pltpu.VMEM((rows, 4 * P_SIZE), jnp.float32),
                pltpu.VMEM((per_owner, rows, rank), jnp.float32),
                pltpu.VMEM((n, width, P_SIZE), jnp.bfloat16),
                pltpu.VMEM((n, width, P_SIZE), jnp.bfloat16),
                pltpu.VMEM((slice_rows, width), jnp.bfloat16),
                pltpu.VMEM((n, slice_rows // n, width), jnp.bfloat16),
                pltpu.VMEM((n, slice_rows // n, width), jnp.bfloat16),
                pltpu.VMEM((lanes, P_SIZE + 8, P_SIZE), jnp.float32),
                pltpu.VMEM((n_seq, lanes, P_SIZE + 8, P_SIZE), jnp.float32),
                dma((5,)),
                dma((2, n // 2, PIECES)),
                dma((2, n // 2, PIECES)),
                dma((n,)),
                dma((n,)),
                dma((n,)),
                dma((n,)),
                dma((n,)),
                dma((n,)),
                dma((n_seq,)),
                dma((n_seq,)),
            ],
            compiler_params=pltpu.CompilerParams(
                collective_id=0, has_side_effects=True, vmem_limit_bytes=58 * 1024 * 1024
            ),
        )(
            span_id,
            prompt_adapter,
            owner_pos,
            slice_len,
            tokens,
            proj_weight,
            pool_down,
            pool_up,
            decay_rate.reshape(1, -1),
            norm_gain.reshape(1, -1),
        )

    in_specs = (
        P("seq", "head"),
        P(None, None, "head"),
        P("head"),
        P("head"),
        P("head", None, None),
        P("head", None, None),
        P(),
        P(),
        P(),
        P(),
    )
    out_specs = (P("seq", "head"), P("seq", None, "head", None))
    return jax.shard_map(body, mesh=mesh, in_specs=in_specs, out_specs=out_specs, check_vma=False)
```

time: 333 us -> 167 us (0.50)
  waiting for transfers between devices: 251 us -> 0 us
  Pallas kernels: 0 us -> 157 us
  matrix products: 26.2 us -> 0 us
  blocking collectives: 19.4 us -> 0 us
  between operations: 15.6 us -> 0.64 us
  other arithmetic: 10.5 us -> 0 us
    all_gather x1 -> x0, waiting for transfers between devices: 163 us -> none  [body(): shard_piece = lax.all_gather(tokens, 'head', axis=1, tiled=True)]
    pallas_call x0 -> x1, Pallas kernels: none -> 157 us  [body(): pl.pallas_call(functools.partial(kernel, n, n_seq), out_shape=(jax.ShapeD...]
    psum x1 -> x0, waiting for transfers between devices: 87.9 us -> none  [broadcast(): return lax.psum(block, axis)]
    dot_general x6 -> x0, matrix products: 26.2 us -> none  [the longest x1 12.3 us: body(): jnp.einsum('td,kdc->tkc', shard_piece, proj_weight, preferred_element_typ...]
    all_gather x3 -> x0, blocking collectives: 19.4 us -> none  [entering(): everything = jax.tree.map(lambda part: lax.all_gather(part, axis), array)]
    unnamed x20 -> x5, local copies, waits for them, and re-layouts: 0.7 us -> 10 us
    mul x7 -> x0, other arithmetic: 3.66 us -> none  [the longest x1 2.51 us: body(): key_decay = key_f * jnp.exp(-cumul)]
    mul x5 -> x0, local copies, waits for them, and re-layouts: 3.55 us -> none  [the longest x4 2.71 us: compose(): factor = late_keep[:, None, None, None] * late_decay[..., None]]
  transfers between devices with their start and end apart: 2 -> 0, of which waited for: 2 -> 0; matrix products, arithmetic and copies ran while one was open for 7% -> 0% of each run, Pallas kernels for 0% -> 0%
where the time goes in v1:
time: 167 us
  Pallas kernels  157 us (94%)
  local copies, waits for them, and re-layouts  10 us (6%)
    pallas_call x1, Pallas kernels, body(): pl.pallas_call(functools.partial(kernel, n, n_seq), out_shape=(jax.ShapeD...  157 us
    unnamed x5, local copies, waits for them, and re-layouts  10 us

profile of v1, /device:TPU:1, one launch (start us, length us, event | category | flops | bytes accessed | tf_op | source)
XLA Modules:
  0.0 167.2 jit_solution(1170383177294066302)
XLA Ops:
  0.6 1.3 copy.12.span_ref
  2.0 1.3 copy.13.len_ref
  3.3 4.1 %copy.14.down_hbm = bf16[2,6144,64]{2,1,0:T(8,128)(2,1)} copy(bf16[2,6144,64]{1,2,0:T(8,128)(2,1)} %param.14) | data formatting | bytes 3145728 | tf_op args[4]
  7.4 156.5 %shard_map.113 = (bf16[1024,128]{1,0:T(8,128)(2,1)}, f32[1,2,128,128]{3,2,1,0:T(8,128)}) custom-call(s32[4,2]{1,0:T(4,128)} %copy.12.span_ref, s32[8]{0:T(128)} %prompt_ref.1, s32[16]{0:T(128)} %owner_ref.1, s32[4,2]{1,0:T(4,128)} %copy.13.len_ref, bf16[1024,768]{1,0:T(8,128)(2,1)} %tok_ref.1, bf16[4,6144,128]{2,1,0:T(8,128)(2,1)} %w_hbm.1, ...), custom_call_target="tpu_custom_call" | custom-call | tf_op jit(solution)/shard_map/pallas_call | solution.py:424
  164.0 1.7 copy.17
  165.6 1.6 copy.18

commit v2 on v1

v2 whole, which is shorter than its diff:
```python
import functools
import math

import jax
import jax.numpy as jnp
from jax import lax
from jax.experimental import pallas as pl
from jax.experimental.pallas import tpu as pltpu
from jax.sharding import PartitionSpec as P

P_SIZE = 128
NORM_FLOOR = 1.0
PIECES = 2
MESH = pl.DeviceIdType.MESH
HIGHEST = lax.Precision.HIGHEST


def grid_of(n):
    across = math.isqrt(n // 2)
    if across >= 2 and 2 * across * across == n:
        return across, n // across
    return 1, n


def head_at(position, n):
    across, depth = grid_of(n)
    if across == 1:
        return position
    width = across - 1
    back = lax.div(lax.div(position, depth) + (across - 1), across)
    rest = (position - depth) * back
    row, step = lax.div(rest, width), lax.rem(rest, width)
    x = 1 + step + lax.rem(row, 2) * (width - 1 - 2 * step)
    return (1 - back) * position * across + back * ((depth - 1 - row) * across + x)


def position_of(head, n):
    across, depth = grid_of(n)
    if across == 1:
        return head
    width = across - 1
    z, x = lax.div(head, across), lax.rem(head, across)
    back = lax.div(x + across - 1, across)
    row, step = depth - 1 - z, (x - 1) * back
    moved = step + lax.rem(row, 2) * (width - 1 - 2 * step)
    return (1 - back) * z + back * (depth + row * width + moved)


def dot(a, b, precision=None):
    return jnp.dot(a, b, preferred_element_type=jnp.float32, precision=precision)


def kernel(
    n,
    n_seq,
    span_ref,
    prompt_ref,
    owner_ref,
    len_ref,
    tok_ref,
    w_hbm,
    down_hbm,
    up_ref,
    rate_ref,
    gain_ref,
    out_ref,
    state_ref,
    slots,
    wbuf,
    dbuf,
    acc,
    up_send,
    up_recv,
    low_send,
    low_recv,
    low_full,
    st_send,
    st_recv,
    w_sem,
    ring_send,
    ring_recv,
    up_ssem,
    up_rsem,
    rs_ssem,
    rs_rsem,
    ag_ssem,
    ag_rsem,
    st_ssem,
    st_rsem,
):
    me = lax.axis_index("head")
    seq = lax.axis_index("seq")
    rows, shard = tok_ref.shape
    lanes = span_ref.shape[0]
    per_owner = down_hbm.shape[0]
    rank = down_hbm.shape[1]
    slice_rows = rows // lanes
    piece = slice_rows // PIECES
    pieces = lanes * PIECES
    half = n // 2
    here = position_of(me, n)
    right = head_at(lax.rem(here + 1, n), n)
    left = head_at(lax.rem(here + n - 1, n), n)
    toward = (right, left)

    loads = [
        pltpu.make_async_copy(w_hbm.at[c], wbuf.at[:, pl.ds(c * P_SIZE, P_SIZE)], w_sem.at[c])
        for c in range(4)
    ]
    loads += [
        pltpu.make_async_copy(down_hbm.at[s], dbuf.at[pl.ds(s * rank, rank)], w_sem.at[4 + s])
        for s in range(per_owner)
    ]

    barrier = pltpu.get_barrier_semaphore()

    def greet_head(d, carry):
        pl.semaphore_signal(
            barrier, inc=1, device_id={"head": lax.rem(me + d, n)}, device_id_type=MESH
        )
        return carry

    def greet_seq(d, carry):
        pl.semaphore_signal(
            barrier, inc=1, device_id={"seq": lax.rem(seq + d, n_seq)}, device_id_type=MESH
        )
        return carry

    lax.fori_loop(1, n, greet_head, 0)
    lax.fori_loop(1, n_seq, greet_seq, 0)
    for load in loads:
        load.start()
    pl.semaphore_wait(barrier, n - 1 + n_seq - 1)

    def hop(direction, step, p, own=False):
        span = pl.ds(p * piece, piece)
        source = tok_ref.at[span] if own else slots.at[direction, step - 2, span]
        return pltpu.make_async_remote_copy(
            src_ref=source,
            dst_ref=slots.at[direction, step - 1, span],
            send_sem=ring_send.at[direction, step - 1, p],
            recv_sem=ring_recv.at[direction, step - 1, p],
            device_id={"head": toward[direction]},
            device_id_type=MESH,
        )

    def long_way(direction, p):
        return p % 2 == direction

    def depart(lane):
        for k in range(PIECES):
            for direction in range(2):
                hop(direction, 1, lane * PIECES + (k + direction) % PIECES, own=True).start()

    depart(0)

    places = [owner_ref[prompt_ref[span_ref[j, seq]]] for j in range(lanes)]
    owned = [
        [jnp.where(places[j] == me * per_owner + s, 1.0, 0.0).astype(jnp.float32) for s in range(per_owner)]
        for j in range(lanes)
    ]

    for j in range(lanes):
        mine = sum(owned[j][s] * up_ref[s].astype(jnp.float32) for s in range(per_owner)).astype(jnp.bfloat16)
        for i in range(n):
            up_send[i, pl.ds(j * rank, rank), :] = mine[:, i * P_SIZE : (i + 1) * P_SIZE]

    def up_copy(d):
        peer = lax.rem(me + d, n)
        return pltpu.make_async_remote_copy(
            src_ref=up_send.at[peer],
            dst_ref=up_recv.at[d],
            send_sem=up_ssem.at[d],
            recv_sem=up_rsem.at[d],
            device_id={"head": peer},
            device_id_type=MESH,
        )

    def up_start(d, carry):
        up_copy(d).start()
        return carry

    lax.fori_loop(1, n, up_start, 0)
    up_recv[0] = up_send[me]

    for load in loads:
        load.wait()

    model = wbuf.shape[0]
    strip = model // 12

    def turn_strip(i, carry):
        deep = pl.ds(pl.multiple_of(i * strip, strip), strip)
        wbuf[deep, pl.ds(4 * P_SIZE, per_owner * rank)] = dbuf[:, deep].T
        return carry

    lax.fori_loop(0, 12, turn_strip, 0)

    def multiply(x, span, origin, first=False):
        deep = pl.ds(pl.multiple_of(origin * shard, 64), shard)
        gained = dot(x, wbuf[deep, :])
        if first:
            acc[span, :] = gained
        else:
            acc[span, :] += gained

    def own_piece(p, carry):
        span = pl.ds(pl.multiple_of(p * piece, piece), piece)
        multiply(tok_ref[span, :], span, me, first=True)
        return carry

    lax.fori_loop(0, pieces, own_piece, 0)

    def arrive(lane, step, forward, present):
        order = [(lane * PIECES + (k + d) % PIECES, d) for k in range(PIECES) for d in range(2)]
        for p, d in order:
            if not present(d, p):
                continue
            own = isinstance(step, int) and step == 1
            hop(d, step, p, own=own).wait_recv()
            if forward(d, p):
                hop(d, step + 1, p).start()
            sign = n - step if d == 0 else step
            origin = head_at(lax.rem(here + sign, n), n)
            span = pl.ds(p * piece, piece)
            multiply(slots[d, step - 1, span, :], span, origin)

    everything = lambda d, p: True
    nothing = lambda d, p: False

    def forwards(step):
        return everything if step < half - 1 else long_way if step == half - 1 else nothing

    def each(count, act):
        def turn(d, carry):
            act(d)
            return carry

        lax.fori_loop(1, count, turn, 0)

    block = slice_rows // n

    def rs_copy(j, d):
        peer = lax.rem(me + d, n)
        return pltpu.make_async_remote_copy(
            src_ref=low_send.at[j, pl.ds(pl.multiple_of(peer * block, block), block)],
            dst_ref=low_recv.at[j, d],
            send_sem=rs_ssem.at[j, d],
            recv_sem=rs_rsem.at[j, d],
            device_id={"head": peer},
            device_id_type=MESH,
        )

    def ag_copy(j, d):
        peer = lax.rem(me + d, n)
        return pltpu.make_async_remote_copy(
            src_ref=low_recv.at[j, 0],
            dst_ref=low_full.at[j, me],
            send_sem=ag_ssem.at[j, d],
            recv_sem=ag_rsem.at[j, d],
            device_id={"head": peer},
            device_id_type=MESH,
        )

    def ag_arrival(j, d):
        peer = lax.rem(me + n - d, n)
        return pltpu.make_async_remote_copy(
            src_ref=low_recv.at[j, 0],
            dst_ref=low_full.at[j, peer],
            send_sem=ag_ssem.at[j, d],
            recv_sem=ag_rsem.at[j, d],
            device_id={"head": peer},
            device_id_type=MESH,
        )

    def st_copy(j, d):
        return pltpu.make_async_remote_copy(
            src_ref=st_send.at[j],
            dst_ref=st_recv.at[j, seq],
            send_sem=st_ssem.at[j, d],
            recv_sem=st_rsem.at[j, d],
            device_id={"seq": lax.rem(seq + d, n_seq)},
            device_id_type=MESH,
        )

    def st_arrival(j, d):
        peer = lax.rem(seq + n_seq - d, n_seq)
        return pltpu.make_async_remote_copy(
            src_ref=st_send.at[j],
            dst_ref=st_recv.at[j, peer],
            send_sem=st_ssem.at[j, d],
            recv_sem=st_rsem.at[j, d],
            device_id={"seq": peer},
            device_id_type=MESH,
        )

    slot_ids = lax.broadcasted_iota(jnp.int32, (slice_rows, 1), 0)

    def causal():
        shape = (slice_rows, slice_rows)
        return lax.broadcasted_iota(jnp.int32, shape, 0) >= lax.broadcasted_iota(jnp.int32, shape, 1)

    def alive(j):
        return jnp.where(slot_ids < len_ref[j, seq], 1.0, 0.0).astype(jnp.float32)

    def low_scatter(j):
        span = pl.ds(j * slice_rows, slice_rows)
        lows = acc[span, pl.ds(4 * P_SIZE, per_owner * rank)]
        mine = sum(owned[j][s] * lows[:, s * rank : (s + 1) * rank] for s in range(per_owner))
        low_send[j] = mine.astype(jnp.bfloat16)
        each(n, lambda d: rs_copy(j, d).start())

    def low_gather(j):
        each(n, lambda d: rs_copy(j, d).wait_recv())
        total = low_send[j, pl.ds(pl.multiple_of(me * block, block), block), :].astype(jnp.float32)
        for d in range(1, n):
            total = total + low_recv[j, d].astype(jnp.float32)
        low_recv[j, 0] = total.astype(jnp.bfloat16)
        each(n, lambda d: ag_copy(j, d).start())
        low_full[j, me] = total.astype(jnp.bfloat16)

    def gates(j):
        span = pl.ds(j * slice_rows, slice_rows)
        up = jnp.sum(up_recv[:, pl.ds(j * rank, rank), :].astype(jnp.float32), axis=0).astype(jnp.bfloat16)
        each(n, lambda d: ag_arrival(j, d).wait_recv())
        gate = acc[span, pl.ds(3 * P_SIZE, P_SIZE)] + dot(low_full[j].reshape(slice_rows, rank), up)
        live = alive(j)
        step_log = -(live * rate_ref[...] * (2.0 * jax.nn.sigmoid(gate)))
        triangle = jnp.where(causal(), 1.0, 0.0).astype(jnp.float32)
        cumul = dot(triangle, step_log, HIGHEST)
        query = acc[span, pl.ds(0, P_SIZE)].astype(jnp.bfloat16).astype(jnp.float32)
        key = acc[span, pl.ds(P_SIZE, P_SIZE)].astype(jnp.bfloat16).astype(jnp.float32) * (
            live * P_SIZE ** (-0.5)
        )
        value = acc[span, pl.ds(2 * P_SIZE, P_SIZE)].astype(jnp.bfloat16).astype(jnp.float32)
        last = cumul[slice_rows - 1 :, :]
        carried = lax.dot_general(
            key * jnp.exp(last - cumul),
            value,
            (((0,), (0,)), ((), ())),
            precision=HIGHEST,
            preferred_element_type=jnp.float32,
        )
        st_send[j, pl.ds(0, P_SIZE), :] = carried
        st_send[j, pl.ds(P_SIZE, 8), :] = jnp.broadcast_to(jnp.exp(last), (8, P_SIZE))
        each(n_seq, lambda d: st_copy(j, d).start())
        st_recv[j, seq] = st_send[j]
        acc[span, pl.ds(0, P_SIZE)] = query * jnp.exp(cumul)
        acc[span, pl.ds(P_SIZE, P_SIZE)] = key * jnp.exp(-cumul)
        acc[span, pl.ds(2 * P_SIZE, P_SIZE)] = value

    def attend(j):
        span = pl.ds(j * slice_rows, slice_rows)
        scores = lax.dot_general(
            acc[span, pl.ds(0, P_SIZE)],
            acc[span, pl.ds(P_SIZE, P_SIZE)],
            (((1,), (1,)), ((), ())),
            precision=HIGHEST,
            preferred_element_type=jnp.float32,
        )
        acc[span, pl.ds(3 * P_SIZE, P_SIZE)] = dot(
            jnp.where(causal(), scores, 0.0), acc[span, pl.ds(2 * P_SIZE, P_SIZE)], HIGHEST
        )

    def finish(j):
        span = pl.ds(j * slice_rows, slice_rows)
        each(n_seq, lambda d: st_arrival(j, d).wait_recv())
        ended = jnp.zeros((P_SIZE, P_SIZE), jnp.float32)
        start = ended
        final = ended
        for k in range(n_seq):
            if k:
                same = jnp.where(span_ref[j, k] == span_ref[j, k - 1], 1.0, 0.0).astype(jnp.float32)
                begun = same * ended
            else:
                begun = ended
            decay = jnp.broadcast_to(st_recv[j, k, pl.ds(P_SIZE, 1), :], (P_SIZE, P_SIZE)).T
            ended = decay * begun + st_recv[j, k, pl.ds(0, P_SIZE), :]
            at = jnp.where(seq == k, 1.0, 0.0).astype(jnp.float32)
            start = start + at * begun
            final = final + at * ended
        inner = acc[span, pl.ds(3 * P_SIZE, P_SIZE)] + dot(acc[span, pl.ds(0, P_SIZE)], start, HIGHEST)
        scale = lax.rsqrt(jnp.maximum(jnp.mean(inner * inner, axis=-1, keepdims=True), NORM_FLOOR))
        out_ref[span, :] = (inner * scale * gain_ref[...] * alive(j)).astype(jnp.bfloat16)
        state_ref[0, j] = final

    stages = (low_scatter, low_gather, gates, attend, finish)
    todo = []
    for j in range(lanes):
        for step in range(1, half + 1):
            if step == half and j + 1 < lanes:
                depart(j + 1)
            arrive(j, step, forwards(step), everything if step < half else long_way)
            if j == 0 and step == half:
                each(n, lambda d: up_copy(d).wait_recv())
            if todo:
                todo.pop(0)()
        while todo:
            todo.pop(0)()
        todo = [functools.partial(stage, j) for stage in stages]
        todo.pop(0)()
    while todo:
        todo.pop(0)()

    each(n, lambda d: up_copy(d).wait_send())
    for j in range(lanes):
        each(n, lambda d: rs_copy(j, d).wait_send())
        each(n, lambda d: ag_copy(j, d).wait_send())
        each(n_seq, lambda d: st_copy(j, d).wait_send())
    for p in range(pieces):
        for direction in range(2):
            hop(direction, 1, p, own=True).wait_send()
    for direction in range(2):
        for p in range(pieces):
            reach = half if long_way(direction, p) else half - 1

            def drained(step, carry):
                hop(direction, step, p).wait_send()
                return carry

            lax.fori_loop(2, reach + 1, drained, 0)


def solution(mesh):
    n, n_seq = mesh.shape["head"], mesh.shape["seq"]

    def body(
        tokens,
        proj_weight,
        decay_rate,
        norm_gain,
        pool_down,
        pool_up,
        span_id,
        prompt_adapter,
        owner_pos,
        slice_len,
    ):
        rows, shard = tokens.shape
        model = proj_weight.shape[1]
        lanes = span_id.shape[1]
        per_owner, _, rank = pool_down.shape
        slice_rows = rows // lanes
        width = lanes * rank
        smem = pl.BlockSpec(memory_space=pltpu.SMEM)
        vmem = pl.BlockSpec(memory_space=pltpu.VMEM)
        hbm = pl.BlockSpec(memory_space=pl.ANY)
        dma = pltpu.SemaphoreType.DMA
        return pl.pallas_call(
            functools.partial(kernel, n, n_seq),
            out_shape=(
                jax.ShapeDtypeStruct((rows, P_SIZE), jnp.bfloat16),
                jax.ShapeDtypeStruct((1, lanes, P_SIZE, P_SIZE), jnp.float32),
            ),
            in_specs=[smem, smem, smem, smem, vmem, hbm, hbm, vmem, vmem, vmem],
            out_specs=(vmem, vmem),
            scratch_shapes=[
                pltpu.VMEM((2, n // 2, rows, shard), jnp.bfloat16),
                pltpu.VMEM((model, 4 * P_SIZE + per_owner * rank), jnp.bfloat16),
                pltpu.VMEM((per_owner * rank, model), jnp.bfloat16),
                pltpu.VMEM((rows, 4 * P_SIZE + per_owner * rank), jnp.float32),
                pltpu.VMEM((n, width, P_SIZE), jnp.bfloat16),
                pltpu.VMEM((n, width, P_SIZE), jnp.bfloat16),
                pltpu.VMEM((lanes, slice_rows, rank), jnp.bfloat16),
                pltpu.VMEM((lanes, n, slice_rows // n, rank), jnp.bfloat16),
                pltpu.VMEM((lanes, n, slice_rows // n, rank), jnp.bfloat16),
                pltpu.VMEM((lanes, P_SIZE + 8, P_SIZE), jnp.float32),
                pltpu.VMEM((lanes, n_seq, P_SIZE + 8, P_SIZE), jnp.float32),
                dma((4 + per_owner,)),
                dma((2, n // 2, lanes * PIECES)),
                dma((2, n // 2, lanes * PIECES)),
                dma((n,)),
                dma((n,)),
                dma((lanes, n)),
                dma((lanes, n)),
                dma((lanes, n)),
                dma((lanes, n)),
                dma((lanes, n_seq)),
                dma((lanes, n_seq)),
            ],
            compiler_params=pltpu.CompilerParams(
                collective_id=0, has_side_effects=True, vmem_limit_bytes=58 * 1024 * 1024
            ),
        )(
            span_id.T,
            prompt_adapter,
            owner_pos,
            slice_len.T,
            tokens,
            proj_weight,
            jnp.swapaxes(pool_down, 1, 2),
            pool_up,
            decay_rate.reshape(1, -1),
            norm_gain.reshape(1, -1),
        )

    in_specs = (
        P("seq", "head"),
        P(None, None, "head"),
        P("head"),
        P("head"),
        P("head", None, None),
        P("head", None, None),
        P(),
        P(),
        P(),
        P(),
    )
    out_specs = (P("seq", "head"), P("seq", None, "head", None))
    return jax.shard_map(body, mesh=mesh, in_specs=in_specs, out_specs=out_specs, check_vma=False)
```

time: 167 us -> 162 us (0.970)
  local copies, waits for them, and re-layouts: 10 us -> 3.24 us
    unnamed x5 -> x2, local copies, waits for them, and re-layouts: 10 us -> 3.24 us
where the time goes in v2:
time: 162 us; the launch traced here: 161 us
  Pallas kernels  158 us (98%)
  local copies, waits for them, and re-layouts  3.24 us (2%)
    pallas_call x1, Pallas kernels, body(): pl.pallas_call(functools.partial(kernel, n, n_seq), out_shape=(jax.ShapeD...  158 us

profile of v2, /device:TPU:1, one launch (start us, length us, event | category | flops | bytes accessed | tf_op | source)
XLA Modules:
  0.0 161.4 jit_solution(12708287503049114574)
XLA Ops:
  0.6 157.5 %shard_map.113 = (bf16[1024,128]{1,0:T(8,128)(2,1)}, f32[1,2,128,128]{3,2,1,0:T(8,128)}) custom-call(s32[2,4]{1,0:T(2,128)} %bitcast.6, s32[8]{0:T(128)} %prompt_ref.1, s32[16]{0:T(128)} %owner_ref.1, s32[2,4]{1,0:T(2,128)} %bitcast.7, bf16[1024,768]{1,0:T(8,128)(2,1)} %tok_ref.1, bf16[4,6144,128]{2,1,0:T(8,128)(2,1)} %w_hbm.1, ...), custom_call_target="tpu_custom_call" | custom-call | tf_op jit(solution)/shard_map/pallas_call | solution.py:449
  158.2 1.7 %copy.14 = bf16[1024,128]{1,0:T(8,128)(2,1)} copy(bf16[1024,128]{1,0:T(8,128)(2,1)} %get-tuple-element.4) | data formatting | bytes 524288
  159.9 1.6 copy.15

commit v3 on v1

--- a/solution.py
+++ b/solution.py
@@ -68,6 +68,7 @@
     slots,
     wbuf,
     dbuf,
+    dturn,
     acc,
     lacc,
     up_send,
@@ -92,9 +93,9 @@
     me = lax.axis_index("head")
     seq = lax.axis_index("seq")
     rows, shard = tok_ref.shape
-    lanes = span_ref.shape[1]
+    lanes = span_ref.shape[0]
     per_owner = down_hbm.shape[0]
-    rank = down_hbm.shape[2]
+    rank = down_hbm.shape[1]
     slice_rows = rows // lanes
     piece = rows // PIECES
     half = n // 2
@@ -107,7 +108,7 @@
         pltpu.make_async_copy(w_hbm.at[c], wbuf.at[:, pl.ds(c * P_SIZE, P_SIZE)], w_sem.at[c])
         for c in range(4)
     ]
-    loads.append(pltpu.make_async_copy(down_hbm, dbuf, w_sem.at[4]))
+    loads.append(pltpu.make_async_copy(down_hbm, dturn, w_sem.at[4]))
 
     barrier = pltpu.get_barrier_semaphore()
 
@@ -148,7 +149,7 @@
         for direction in range(2):
             hop(direction, 1, (k + direction) % PIECES, own=True).start()
 
-    places = [owner_ref[prompt_ref[span_ref[seq, j]]] for j in range(lanes)]
+    places = [owner_ref[prompt_ref[span_ref[j, seq]]] for j in range(lanes)]
     owned = [
         [jnp.where(places[j] == me * per_owner + s, 1.0, 0.0).astype(jnp.float32) for s in range(per_owner)]
         for j in range(lanes)
@@ -179,6 +180,16 @@
 
     for load in loads:
         load.wait()
+
+    strip = wbuf.shape[0] // 12
+
+    def turn_strip(i, carry):
+        deep = pl.ds(pl.multiple_of(i * strip, strip), strip)
+        for s in range(per_owner):
+            dbuf[s, deep, :] = dturn[s, :, deep].T
+        return carry
+
+    lax.fori_loop(0, 12, turn_strip, 0)
 
     def multiply(x, span, origin, first=False):
         deep = pl.ds(pl.multiple_of(origin * shard, 64), shard)
@@ -299,7 +310,7 @@
         span = pl.ds(j * slice_rows, slice_rows)
         own = (columns >= j * rank) & (columns < (j + 1) * rank)
         gate = acc[span, pl.ds(3 * P_SIZE, P_SIZE)] + dot(jnp.where(own, low, 0.0).astype(jnp.bfloat16), up)
-        live = jnp.where(slot_ids < len_ref[seq, j], 1.0, 0.0).astype(jnp.float32)
+        live = jnp.where(slot_ids < len_ref[j, seq], 1.0, 0.0).astype(jnp.float32)
         step_log = -(live * rate_ref[...] * (2.0 * jax.nn.sigmoid(gate)))
         cumul = dot(triangle, step_log, HIGHEST)
         query = acc[span, pl.ds(0, P_SIZE)].astype(jnp.bfloat16).astype(jnp.float32)
@@ -364,7 +375,7 @@
         final = ended
         for k in range(n_seq):
             if k:
-                same = jnp.where(span_ref[k, j] == span_ref[k - 1, j], 1.0, 0.0).astype(jnp.float32)
+                same = jnp.where(span_ref[j, k] == span_ref[j, k - 1], 1.0, 0.0).astype(jnp.float32)
                 begun = same * ended
             else:
                 begun = ended
@@ -433,6 +444,7 @@
                 pltpu.VMEM((2, n // 2, rows, shard), jnp.bfloat16),
                 pltpu.VMEM((model, 4 * P_SIZE), jnp.bfloat16),
                 pltpu.VMEM((per_owner, model, rank), jnp.bfloat16),
+                pltpu.VMEM((per_owner, rank, model), jnp.bfloat16),
                 pltpu.VMEM((rows, 4 * P_SIZE), jnp.float32),
                 pltpu.VMEM((per_owner, rows, rank), jnp.float32),
                 pltpu.VMEM((n, width, P_SIZE), jnp.bfloat16),
@@ -458,13 +470,13 @@
                 collective_id=0, has_side_effects=True, vmem_limit_bytes=58 * 1024 * 1024
             ),
         )(
-            span_id,
+            span_id.T,
             prompt_adapter,
             owner_pos,
-            slice_len,
+            slice_len.T,
             tokens,
             proj_weight,
-            pool_down,
+            jnp.swapaxes(pool_down, 1, 2),
             pool_up,
             decay_rate.reshape(1, -1),
             norm_gain.reshape(1, -1),

time: 167 us -> 161 us (0.964)
  local copies, waits for them, and re-layouts: 10 us -> 3.24 us
    unnamed x5 -> x2, local copies, waits for them, and re-layouts: 10 us -> 3.24 us
where the time goes in v3:
time: 161 us; the launch traced here: 160 us
  Pallas kernels  157 us (98%)
  local copies, waits for them, and re-layouts  3.24 us (2%)
    pallas_call x1, Pallas kernels, body(): pl.pallas_call(functools.partial(kernel, n, n_seq), out_shape=(jax.ShapeD...  157 us
    unnamed x2, local copies, waits for them, and re-layouts  3.24 us

profile of v3, /device:TPU:1, one launch (start us, length us, event | category | flops | bytes accessed | tf_op | source)
XLA Modules:
  0.0 160.4 jit_solution(8118518317540957751)
XLA Ops:
  0.6 156.5 %shard_map.113 = (bf16[1024,128]{1,0:T(8,128)(2,1)}, f32[1,2,128,128]{3,2,1,0:T(8,128)}) custom-call(s32[2,4]{1,0:T(2,128)} %bitcast.6, s32[8]{0:T(128)} %prompt_ref.1, s32[16]{0:T(128)} %owner_ref.1, s32[2,4]{1,0:T(2,128)} %bitcast.7, bf16[1024,768]{1,0:T(8,128)(2,1)} %tok_ref.1, bf16[4,6144,128]{2,1,0:T(8,128)(2,1)} %w_hbm.1, ...), custom_call_target="tpu_custom_call" | custom-call | tf_op jit(solution)/shard_map/pallas_call | solution.py:435
  157.1 1.7 %copy.14 = bf16[1024,128]{1,0:T(8,128)(2,1)} copy(bf16[1024,128]{1,0:T(8,128)(2,1)} %get-tuple-element.4) | data formatting | bytes 524288
  158.8 1.6 copy.15
